TPU v7x, 32 devices: a whole 2x2x4 slice. The times are simulated.
32 devices in a mesh: expert: 8 (over z, x), tensor: 4 (over y, core).
Axes of the slice: x: 2, y: 2, z: 4, core: 2. Of those that a mesh axis runs over, the one named last changes fastest.
Arguments:
- tokens: bfloat16 [512, 8192], P('expert', 'tensor'), may hold values from -6 to 6
- frozen_gate_weight: bfloat16 [8192, 28672], P('tensor', 'expert'), may hold values from -0.0625 to 0.0625
- frozen_up_weight: bfloat16 [8192, 28672], P('tensor', 'expert'), may hold values from -0.0625 to 0.0625
- frozen_down_weight: bfloat16 [28672, 8192], P('expert', 'tensor'), may hold values from -0.03125 to 0.03125
- adapter_down_weight: bfloat16 [32, 8192, 128], P('expert', 'tensor'), may hold values from -0.0625 to 0.0625
- adapter_up_weight: bfloat16 [32, 128, 8192], P('expert', None, 'tensor'), may hold values from -0.0625 to 0.0625
- routes: int32 [512, 2], P('expert'), may hold values from 0 to 31, all different within a row; in each aligned block of 64 rows (0 to 63, 64 to 127, ...) at most 8 rows name the same one
- route_gate_weights: float32 [512, 2], P('expert'), may hold values from 0.1 to 1
- output_gradient: bfloat16 [512, 8192], P('expert', 'tensor'), may hold values from -6 to 6
Outputs:
- ffn_out: bfloat16 [512, 8192], P('expert', 'tensor')
- grad_down: bfloat16 [32, 8192, 128], P('expert', 'tensor')
- grad_up: bfloat16 [32, 128, 8192], P('expert', None, 'tensor')
Inputs may be any that keep to these rules, and one draw needn't show every extreme that they name: `routes`: the two experts of a token differ. Among the 64 rows of one index of expert no expert is named more than 8 times, and in some such rows one expert is named exactly 8 times.
All inputs are finite; a program needn't handle non-finite values.
Results may differ from a plain program's by a relative error of at most 0.025.
Values may be sent and summed in bfloat16 or wider, within the bound.
A program may use at most 128 MiB of HBM per device.

v0:
```python
import jax
import jax.numpy as jnp
from jax import lax
from jax.sharding import PartitionSpec as P

F32 = jnp.float32
BF16 = jnp.bfloat16


def activate(gate_part, up_part):
    return (jax.nn.silu(gate_part) * up_part).astype(BF16)


def frozen_layer(shard_rows, gate_weight, up_weight, down_weight):
    hidden_width = gate_weight.shape[1]
    gate_part = jnp.dot(shard_rows, gate_weight, preferred_element_type=F32).astype(BF16)
    up_part = jnp.dot(shard_rows, up_weight, preferred_element_type=F32).astype(BF16)
    summed = lax.psum_scatter(
        jnp.concatenate([gate_part, up_part], axis=1), "tensor", scatter_dimension=0, tiled=True
    ).astype(F32)
    hidden = activate(summed[:, :hidden_width], summed[:, hidden_width:])
    hidden_all = lax.all_gather(hidden, "tensor", axis=0, tiled=True)
    return jnp.dot(hidden_all, down_weight, preferred_element_type=F32)


def per_device(
    tokens,
    frozen_gate_weight,
    frozen_up_weight,
    frozen_down_weight,
    adapter_down_weight,
    adapter_up_weight,
    routes,
    route_gate_weights,
    output_gradient,
):
    n_expert = lax.axis_size("expert")
    tok_count, width_part = tokens.shape
    resident = adapter_down_weight.shape[0]
    most_slots = max(2, 4 * tok_count // (resident * n_expert))
    capacity = most_slots * n_expert
    total = tok_count * n_expert
    shard_rows = lax.all_gather(tokens, "expert", axis=0, tiled=True)
    meta = jnp.concatenate([routes.T.astype(F32), route_gate_weights.T], axis=0)
    meta_all = lax.all_gather(meta, "expert", axis=1, tiled=True)
    grad_rows = lax.all_gather(output_gradient, "expert", axis=0, tiled=True)
    local = (lax.axis_index("expert") * resident + jnp.arange(resident)).astype(F32)
    hit_0 = meta_all[0][None, :] == local[:, None]
    hit_1 = meta_all[1][None, :] == local[:, None]
    member = hit_0 | hit_1
    weight = jnp.where(hit_0, meta_all[2][None, :], 0.0) + jnp.where(
        hit_1, meta_all[3][None, :], 0.0
    )
    span = jnp.arange(tok_count)
    before = (span[:, None] < span[None, :]).astype(BF16)
    rank = jnp.dot(
        member.astype(BF16).reshape(resident * n_expert, tok_count),
        before,
        preferred_element_type=F32,
    ).reshape(resident, total)
    base_slot = (jnp.arange(total) // tok_count * most_slots).astype(F32)
    slot = jnp.where(member, rank + base_slot[None, :], -1.0)
    select = slot[:, None, :] == jnp.arange(capacity, dtype=F32)[None, :, None]
    slot_weight = jnp.sum(jnp.where(select, weight[:, None, :], 0.0), axis=2)
    pick = select.astype(BF16).reshape(resident * capacity, total)
    inputs = jnp.dot(pick, shard_rows, preferred_element_type=F32).astype(BF16)
    inputs = inputs.reshape(resident, capacity, width_part)
    cotangents = jnp.dot(pick, grad_rows, preferred_element_type=F32)
    scaled = (slot_weight[:, :, None] * cotangents.reshape(resident, capacity, width_part)).astype(
        BF16
    )
    low_part = jnp.einsum(
        "ecw,ewr->ecr", inputs, adapter_down_weight, preferred_element_type=F32
    ).astype(BF16)
    back_part = jnp.einsum(
        "ecw,erw->ecr", scaled, adapter_up_weight, preferred_element_type=F32
    ).astype(BF16)
    both = lax.psum(jnp.concatenate([low_part, back_part], axis=2), "tensor")
    rank_width = low_part.shape[2]
    low, back = (both[:, :, :rank_width], both[:, :, rank_width:])
    grad_up = jnp.einsum("ecr,ecw->erw", low, scaled, preferred_element_type=F32).astype(BF16)
    grad_down = jnp.einsum("ecw,ecr->ewr", inputs, back, preferred_element_type=F32).astype(BF16)
    rows = jnp.einsum("ecr,erw->ecw", low, adapter_up_weight, preferred_element_type=F32)
    rows = (slot_weight[:, :, None] * rows).astype(BF16).reshape(resident * capacity, width_part)
    adapter_part = lax.dot_general(pick, rows, (((0,), (0,)), ((), ())), preferred_element_type=F32)
    base_part = frozen_layer(shard_rows, frozen_gate_weight, frozen_up_weight, frozen_down_weight)
    ffn_out = lax.psum_scatter(
        (base_part + adapter_part).astype(BF16), "expert", scatter_dimension=0, tiled=True
    )
    return (ffn_out, grad_down, grad_up)


def solution(mesh):
    placed = (
        P("expert", "tensor"),
        P("tensor", "expert"),
        P("tensor", "expert"),
        P("expert", "tensor"),
        P("expert", "tensor", None),
        P("expert", None, "tensor"),
        P("expert", None),
        P("expert", None),
        P("expert", "tensor"),
    )
    return jax.shard_map(
        per_device,
        mesh=mesh,
        in_specs=placed,
        out_specs=(P("expert", "tensor"), P("expert", "tensor", None), P("expert", None, "tensor")),
        check_vma=False,
    )
```

profile of v0, /device:TPU:0, one launch (start us, length us, event | category | flops | bytes accessed | tf_op | source)
XLA Modules:
  0.0 358.7 jit_solution(514019846233866210)
XLA Ops:
  7.2 0.7 all-gather.5.cloned.1.call-update
  8.0 54.0 %all-gather.5.cloned.1.call-done = bf16[512,2048]{1,0:T(8,128)(2,1)} async-done(((bf16[64,2048]{1,0:T(8,128)(2,1)}), bf16[512,2048]{1,0:T(8,128)(2,1)}) %all-gather.5.cloned.1.call-update) | async-done | bytes 2097168 | tf_op jit(solution)/shard_map/all_gather | solution.py:43
  62.0 14.9 %convolution_convert_fusion = bf16[512,3584]{1,0:T(8,128)(2,1)} fusion(bf16[512,2048]{1,0:T(8,128)(2,1)} %all-gather.5.cloned.1.call-done, bf16[2048,3584]{1,0:T(8,128)(2,1)} %param.11), kind=kOutput, calls=%fused_computation.1 | convolution fusion | flops 7518027776 | bytes 20447232 | tf_op jit(solution)/shard_map/dot_general | solution.py:17
  76.9 12.4 %convolution_convert_fusion.1 = bf16[512,3584]{1,0:T(8,128)(2,1)} fusion(bf16[512,2048]{1,0:T(8,128)(2,1)S(1)} %copy-done.4, bf16[2048,3584]{1,0:T(8,128)(2,1)} %param.10), kind=kOutput, calls=%fused_computation.2 | convolution fusion | flops 7518027776 | bytes 20447232 | tf_op jit(solution)/shard_map/dot_general | solution.py:16
  89.3 6.9 %pad_maximum_fusion = bf16[512,7168]{1,0:T(8,128)(2,1)} fusion(bf16[512,3584]{1,0:T(8,128)(2,1)} %convolution_convert_fusion, bf16[512,3584]{1,0:T(8,128)(2,1)} %convolution_convert_fusion.1), kind=kLoop, calls=%fused_computation | loop fusion | flops 14680064 | bytes 14680064 | tf_op jit(solution)/shard_map/concatenate | solution.py:19
  96.2 0.7 all-gather.9.cloned.1.call-update
  96.9 63.8 %reduce-scatter.3.cloned.1.call-done = bf16[128,7168]{1,0:T(8,128)(2,1)} async-done(((bf16[512,7168]{1,0:T(8,128)(2,1)}), bf16[128,7168]{1,0:T(8,128)(2,1)}) %reduce-scatter.3.cloned.1.call-update) | async-done | bytes 1835024 | tf_op jit(solution)/shard_map/reduce_scatter | solution.py:18
  160.8 1.9 convert_element_type.61
  162.7 1.4 fusion.4
  164.2 26.2 %all-gather = f32[8,64,4]{1,2,0:T(4,128)S(1)} all-gather(f32[1,64,4]{1,2,0:T(4,128)S(1)} %maximum_bitcast_fusion), channel_id=1, replica_groups=mesh['expert'=8,'tensor'=4] {'expert'}, dimensions={0}, use_global_device_ids=true | all-gather | bytes 9216 | tf_op jit(solution)/shard_map/all_gather | solution.py:45
  190.4 0.1 reshape.195
  190.7 0.1 eq.102
  190.9 0.2 fusion.12
  191.1 0.1 eq.114
  191.3 0.1 bitcast_compare_fusion
  191.5 0.1 select_reduce_fusion
  191.6 2.3 convolution_convert_fusion.4
  193.9 18.2 %all-gather.9.cloned.1.call-done = bf16[512,2048]{1,0:T(8,128)(2,1)} async-done(((bf16[64,2048]{1,0:T(8,128)(2,1)}), bf16[512,2048]{1,0:T(8,128)(2,1)}) %all-gather.9.cloned.1.call-update) | async-done | bytes 2097168 | tf_op jit(solution)/shard_map/all_gather | solution.py:46
  212.1 2.3 fusion.1
  214.4 0.8 convolution_convert_fusion.5
  215.3 1.1 copy-done.3
  216.4 0.5 convolution_convert_fusion.6
  216.9 0.7 pad_maximum_fusion.1
  217.6 0.2 reduce-scatter.5.cloned.1.call-start
  217.9 26.3 %all-gather.7.cloned.1.call-done = bf16[512,3584]{1,0:T(8,128)(2,1)} async-done(((bf16[128,3584]{1,0:T(8,128)(2,1)}), bf16[512,3584]{1,0:T(8,128)(2,1)}) %all-gather.7.cloned.1.call-update) | async-done | bytes 3670032 | tf_op jit(solution)/shard_map/all_gather | solution.py:22
  244.1 13.5 %fusion.24 = f32[512,2048]{1,0:T(8,128)} fusion(bf16[512,3584]{1,0:T(8,128)(2,1)} %all-gather.7.cloned.1.call-done, bf16[3584,2048]{1,0:T(8,128)(2,1)} %param.12), kind=kOutput, calls=%fused_computation.54 | convolution fusion | flops 7516192768 | bytes 22544384 | tf_op jit(solution)/shard_map/dot_general | solution.py:23
  257.6 21.1 %all-reduce.2.cloned.1.call-done = bf16[4,64,256]{2,1,0:T(8,128)(2,1)} async-done(((bf16[4,64,256]{2,1,0:T(8,128)(2,1)}), bf16[4,64,256]{2,1,0:T(8,128)(2,1)}) %all-reduce.2.cloned.1.call-update) | async-done | bytes 131088 | tf_op jit(solution)/shard_map/psum | solution.py:78
  278.7 4.6 %fusion = bf16[512,2048]{1,0:T(8,128)(2,1)} fusion(f32[512,2048]{1,0:T(8,128)} %fusion.24, bf16[4,128,2048]{2,1,0:T(8,128)(2,1)S(1)} %copy-done, f32[4,64]{1,0:T(4,128)S(1)} %select_reduce_fusion, f32[4,512]{1,0:T(4,128)S(1)} %get-tuple-element.9, bf16[4,64,256]{2,1,0:T(8,128)(2,1)} %all-reduce.2.cloned.1.call-done), kind=kOutput, calls=%fused_computation.4 | convolution fusion | flops 674365440 | bytes 8463360 | tf_op jit(solution)/shard_map/dot_general | solution.py:85
  283.3 0.9 copy-done.5
  284.2 2.2 convolution_convert_fusion.3
  286.4 2.1 convolution_convert_fusion.2
  288.5 63.4 %reduce-scatter.5.cloned.1.call-done = bf16[64,2048]{1,0:T(8,128)(2,1)} async-done(((bf16[512,2048]{1,0:T(8,128)(2,1)}), bf16[64,2048]{1,0:T(8,128)(2,1)}) %reduce-scatter.5.cloned.1.call-update) | async-done | bytes 262160 | tf_op jit(solution)/shard_map/reduce_scatter | solution.py:87
  (35 shorter events, 0.7 us)
Async XLA Ops:
  7.2 207.2 %copy-start = (bf16[4,128,2048]{2,1,0:T(8,128)(2,1)S(1)}, bf16[4,128,2048]{2,1,0:T(8,128)(2,1)}, u32[]{:S(2)}) copy-start(bf16[4,128,2048]{2,1,0:T(8,128)(2,1)} %param.14) | copy-start | bytes 6291460
  7.2 54.8 %all-gather.5.cloned.1.call-start = ((), (), s32[]{:S(2)}) async-start(), calls=%async_computation.2 | async-start | bytes 2359296 | tf_op jit(solution)/shard_map/all_gather | solution.py:43
  7.9 152.9 %reduce-scatter.3.cloned.1.call-start = ((), (), s32[]{:S(2)}) async-start(), calls=%async_computation.3 | async-start | bytes 9175040 | tf_op jit(solution)/shard_map/reduce_scatter | solution.py:18
  62.0 15.0 %copy-start.4 = (bf16[512,2048]{1,0:T(8,128)(2,1)S(1)}, bf16[512,2048]{1,0:T(8,128)(2,1)}, u32[]{:S(2)}) copy-start(bf16[512,2048]{1,0:T(8,128)(2,1)} %all-gather.5.cloned.1.call-done) | copy-start | bytes 6291460
  96.2 115.9 %all-gather.9.cloned.1.call-start = ((), (), s32[]{:S(2)}) async-start(), calls=%async_computation.5 | async-start | bytes 2359296 | tf_op jit(solution)/shard_map/all_gather | solution.py:46
  96.9 147.2 %all-gather.7.cloned.1.call-start = ((), (), s32[]{:S(2)}) async-start(), calls=%async_computation.4 | async-start | bytes 4587520 | tf_op jit(solution)/shard_map/all_gather | solution.py:22
  162.7 1.5 copy-start.6
  162.7 1.5 copy-start.7
  164.1 114.5 %all-reduce.2.cloned.1.call-start = ((), (), s32[]{:S(2)}) async-start(), calls=%async_computation.6 | async-start | bytes 262144 | tf_op jit(solution)/shard_map/psum | solution.py:78
  214.4 2.5 copy-start.1
  214.4 2.0 copy-start.3
  217.6 134.2 %reduce-scatter.5.cloned.1.call-start = ((), (), s32[]{:S(2)}) async-start(), calls=%async_computation.7 | async-start | bytes 2359296 | tf_op jit(solution)/shard_map/reduce_scatter | solution.py:87
  283.3 0.9 copy-start.5
  284.2 2.2 copy-start.2
Sparse Core Ops, SparseCore 0:
  10.1 51.7 all-gather.4
  96.3 64.4 reduce-scatter.2
  162.9 49.1 all-gather.8
  214.1 30.0 all-gather.6
  246.9 31.7 all-reduce.1
  283.4 68.3 reduce-scatter.4
where the time goes:
time: 359 us
  waiting for transfers between devices  248 us (69%)
  matrix products  55.8 us (16%)
  blocking collectives  26.2 us (7%)
  between operations  14.3 us (4%)
  other arithmetic  11.2 us (3%)
    reduce_scatter x1, waiting for transfers between devices, frozen_layer(): lax.psum_scatter(jnp.concatenate([gate_part, up_part], axis=1), 'tensor',...  63.8 us
    reduce_scatter x1, waiting for transfers between devices, per_device(): lax.psum_scatter((base_part + adapter_part).astype(BF16), 'expert', scatt...  63.4 us
    all_gather x1, waiting for transfers between devices, per_device(): shard_rows = lax.all_gather(tokens, 'expert', axis=0, tiled=True)  54 us
    all_gather x1, waiting for transfers between devices, frozen_layer(): hidden_all = lax.all_gather(hidden, 'tensor', axis=0, tiled=True)  26.3 us
    all_gather x1, blocking collectives, per_device(): meta_all = lax.all_gather(meta, 'expert', axis=1, tiled=True)  26.2 us
    psum x1, waiting for transfers between devices, per_device(): both = lax.psum(jnp.concatenate([low_part, back_part], axis=2), 'tensor')  21.1 us
    all_gather x1, waiting for transfers between devices, per_device(): grad_rows = lax.all_gather(output_gradient, 'expert', axis=0, tiled=True)  18.2 us
    dot_general x1, matrix products, frozen_layer(): jnp.dot(shard_rows, up_weight, preferred_element_type=F32).astype(BF16)  14.9 us
  transfers between devices with their start and end apart: 6, of which 6 were waited for; matrix products, arithmetic and copies ran while one was open for 8% of the time, Pallas kernels for 0%

commit v1 on v0

--- a/solution.py
+++ b/solution.py
@@ -42,7 +42,17 @@
     total = tok_count * n_expert
     shard_rows = lax.all_gather(tokens, "expert", axis=0, tiled=True)
     meta = jnp.concatenate([routes.T.astype(F32), route_gate_weights.T], axis=0)
-    meta_all = lax.all_gather(meta, "expert", axis=1, tiled=True)
+    value = meta
+    ways, here, step = (lax.axis_size("expert"), lax.axis_index("expert"), value.shape[1])
+    lengths = [n * ways if d == 1 else n for d, n in enumerate(value.shape)]
+    meta_all = lax.dynamic_update_slice_in_dim(
+        jnp.zeros(lengths, value.dtype), value, here * step, axis=1
+    )
+    for far in range(1, ways):
+        value = lax.ppermute(value, "expert", [(d, (d + 1) % ways) for d in range(ways)])
+        meta_all = lax.dynamic_update_slice_in_dim(
+            meta_all, value, (here - far) % ways * step, axis=1
+        )
     grad_rows = lax.all_gather(output_gradient, "expert", axis=0, tiled=True)
     local = (lax.axis_index("expert") * resident + jnp.arange(resident)).astype(F32)
     hit_0 = meta_all[0][None, :] == local[:, None]

time: 359 us -> 359 us (level)
  blocking collectives: 26.2 us -> 0 us
  waiting for transfers between devices: 248 us -> 272 us
    ppermute x0 -> x7, waiting for transfers between devices: none -> 41.1 us  [per_device(): lax.ppermute(value, 'expert', [(d, (d + 1) % ways) for d in range(ways)])]
    all_gather x1 -> x0, blocking collectives: 26.2 us -> none  [per_device(): meta_all = lax.all_gather(meta, 'expert', axis=1, tiled=True)]
    all_gather x1, waiting for transfers between devices: 18.2 us -> 0.67 us  [per_device(): grad_rows = lax.all_gather(output_gradient, 'expert', axis=0, tiled=True)]
  transfers between devices with their start and end apart: 6 -> 13, of which waited for: 6 -> 13; matrix products, arithmetic and copies ran while one was open for 8% -> 8% of each run, Pallas kernels for 0% -> 0%
where the time goes in v1:
time: 359 us
  waiting for transfers between devices  272 us (76%)
  matrix products  55.8 us (16%)
  between operations  14.3 us (4%)
  other arithmetic  11.2 us (3%)
  local copies, waits for them, and re-layouts  4.03 us (1%)
    reduce_scatter x1, waiting for transfers between devices, frozen_layer(): lax.psum_scatter(jnp.concatenate([gate_part, up_part], axis=1), 'tensor',...  63.9 us
    reduce_scatter x1, waiting for transfers between devices, per_device(): lax.psum_scatter((base_part + adapter_part).astype(BF16), 'expert', scatt...  63.5 us
    all_gather x1, waiting for transfers between devices, per_device(): shard_rows = lax.all_gather(tokens, 'expert', axis=0, tiled=True)  54 us
    ppermute x7, waiting for transfers between devices, per_device(): lax.ppermute(value, 'expert', [(d, (d + 1) % ways) for d in range(ways)])  41.1 us
    all_gather x1, waiting for transfers between devices, frozen_layer(): hidden_all = lax.all_gather(hidden, 'tensor', axis=0, tiled=True)  26.3 us
    psum x1, waiting for transfers between devices, per_device(): both = lax.psum(jnp.concatenate([low_part, back_part], axis=2), 'tensor')  21.1 us
    dot_general x1, matrix products, frozen_layer(): jnp.dot(shard_rows, up_weight, preferred_element_type=F32).astype(BF16)  15 us
    dot_general x1, matrix products, frozen_layer(): return jnp.dot(hidden_all, down_weight, preferred_element_type=F32)  13.4 us
  transfers between devices with their start and end apart: 13, of which 13 were waited for; matrix products, arithmetic and copies ran while one was open for 8% of the time, Pallas kernels for 0%

profile of v1, /device:TPU:0, one launch (start us, length us, event | category | flops | bytes accessed | tf_op | source)
XLA Modules:
  0.0 359.2 jit_solution(4823874996972786184)
XLA Ops:
  7.2 0.7 all-gather.4.cloned.1.call-update
  8.0 54.0 %all-gather.4.cloned.1.call-done = bf16[512,2048]{1,0:T(8,128)(2,1)} async-done(((bf16[64,2048]{1,0:T(8,128)(2,1)}), bf16[512,2048]{1,0:T(8,128)(2,1)}) %all-gather.4.cloned.1.call-update) | async-done | bytes 2097168 | tf_op jit(solution)/shard_map/all_gather | solution.py:43
  62.0 15.0 %convolution_convert_fusion = bf16[512,3584]{1,0:T(8,128)(2,1)} fusion(bf16[512,2048]{1,0:T(8,128)(2,1)} %all-gather.4.cloned.1.call-done, bf16[2048,3584]{1,0:T(8,128)(2,1)} %param.11), kind=kOutput, calls=%fused_computation.1 | convolution fusion | flops 7518027776 | bytes 20447232 | tf_op jit(solution)/shard_map/dot_general | solution.py:17
  76.9 12.4 %convolution_convert_fusion.1 = bf16[512,3584]{1,0:T(8,128)(2,1)} fusion(bf16[512,2048]{1,0:T(8,128)(2,1)S(1)} %copy-done.4, bf16[2048,3584]{1,0:T(8,128)(2,1)} %param.10), kind=kOutput, calls=%fused_computation.2 | convolution fusion | flops 7518027776 | bytes 20447232 | tf_op jit(solution)/shard_map/dot_general | solution.py:16
  89.3 6.9 %pad_maximum_fusion = bf16[512,7168]{1,0:T(8,128)(2,1)} fusion(bf16[512,3584]{1,0:T(8,128)(2,1)} %convolution_convert_fusion, bf16[512,3584]{1,0:T(8,128)(2,1)} %convolution_convert_fusion.1), kind=kLoop, calls=%fused_computation | loop fusion | flops 14680064 | bytes 14680064 | tf_op jit(solution)/shard_map/concatenate | solution.py:19
  96.2 0.7 all-gather.8.cloned.1.call-update
  97.0 63.9 %reduce-scatter.3.cloned.1.call-done = bf16[128,7168]{1,0:T(8,128)(2,1)} async-done(((bf16[512,7168]{1,0:T(8,128)(2,1)}), bf16[128,7168]{1,0:T(8,128)(2,1)}) %reduce-scatter.3.cloned.1.call-update) | async-done | bytes 1835024 | tf_op jit(solution)/shard_map/reduce_scatter | solution.py:18
  160.9 1.9 convert_element_type.61
  162.7 1.4 fusion.4
  164.3 1.5 collective-permute-start
  165.8 4.8 %collective-permute-done = f32[4,64]{1,0:T(4,128)S(1)} collective-permute-done((f32[4,64]{1,0:T(4,128)S(1)}, f32[4,64]{1,0:T(4,128)S(1)}, u32[]{:S(2)}, u32[]{:S(2)}) %collective-permute-start) | collective-permute-done | bytes 1056 | tf_op jit(solution)/shard_map/ppermute | solution.py:52
  170.6 6.3 %collective-permute-done.1 = f32[4,64]{1,0:T(4,128)S(1)} collective-permute-done((f32[4,64]{1,0:T(4,128)S(1)}, f32[4,64]{1,0:T(4,128)S(1)}, u32[]{:S(2)}, u32[]{:S(2)}) %collective-permute-start.1) | collective-permute-done | bytes 1056 | tf_op jit(solution)/shard_map/ppermute | solution.py:52
  176.9 6.3 %collective-permute-done.2 = f32[4,64]{1,0:T(4,128)S(1)} collective-permute-done((f32[4,64]{1,0:T(4,128)S(1)}, f32[4,64]{1,0:T(4,128)S(1)}, u32[]{:S(2)}, u32[]{:S(2)}) %collective-permute-start.2) | collective-permute-done | bytes 1056 | tf_op jit(solution)/shard_map/ppermute | solution.py:52
  183.2 6.3 %collective-permute-done.3 = f32[4,64]{1,0:T(4,128)S(1)} collective-permute-done((f32[4,64]{1,0:T(4,128)S(1)}, f32[4,64]{1,0:T(4,128)S(1)}, u32[]{:S(2)}, u32[]{:S(2)}) %collective-permute-start.3) | collective-permute-done | bytes 1056 | tf_op jit(solution)/shard_map/ppermute | solution.py:52
  189.5 6.3 %collective-permute-done.4 = f32[4,64]{1,0:T(4,128)S(1)} collective-permute-done((f32[4,64]{1,0:T(4,128)S(1)}, f32[4,64]{1,0:T(4,128)S(1)}, u32[]{:S(2)}, u32[]{:S(2)}) %collective-permute-start.4) | collective-permute-done | bytes 1056 | tf_op jit(solution)/shard_map/ppermute | solution.py:52
  195.8 6.5 %collective-permute-done.5 = f32[4,64]{1,0:T(4,128)S(1)} collective-permute-done((f32[4,64]{1,0:T(4,128)S(1)}, f32[4,64]{1,0:T(4,128)S(1)}, u32[]{:S(2)}, u32[]{:S(2)}) %collective-permute-start.5) | collective-permute-done | bytes 1056 | tf_op jit(solution)/shard_map/ppermute | solution.py:52
  203.9 4.7 %collective-permute-done.6 = f32[4,64]{1,0:T(4,128)S(1)} collective-permute-done((f32[4,64]{1,0:T(4,128)S(1)}, f32[4,64]{1,0:T(4,128)S(1)}, u32[]{:S(2)}, u32[]{:S(2)}) %collective-permute-start.6) | collective-permute-done | bytes 1056 | tf_op jit(solution)/shard_map/ppermute | solution.py:52
  209.6 2.3 convolution_convert_fusion.4
  211.9 0.7 all-gather.8.cloned.1.call-done
  212.6 2.3 fusion.1
  214.9 0.8 convolution_convert_fusion.5
  215.7 1.1 copy-done.3
  216.9 0.5 convolution_convert_fusion.6
  217.4 0.7 pad_maximum_fusion.1
  218.1 26.3 %all-gather.6.cloned.1.call-done = bf16[512,3584]{1,0:T(8,128)(2,1)} async-done(((bf16[128,3584]{1,0:T(8,128)(2,1)}), bf16[512,3584]{1,0:T(8,128)(2,1)}) %all-gather.6.cloned.1.call-update) | async-done | bytes 3670032 | tf_op jit(solution)/shard_map/all_gather | solution.py:22
  244.5 13.4 %fusion.24 = f32[512,2048]{1,0:T(8,128)} fusion(bf16[512,3584]{1,0:T(8,128)(2,1)} %all-gather.6.cloned.1.call-done, bf16[3584,2048]{1,0:T(8,128)(2,1)} %param.12), kind=kOutput, calls=%fused_computation.54 | convolution fusion | flops 7516192768 | bytes 22544384 | tf_op jit(solution)/shard_map/dot_general | solution.py:23
  257.9 21.1 %all-reduce.2.cloned.1.call-done = bf16[4,64,256]{2,1,0:T(8,128)(2,1)} async-done(((bf16[4,64,256]{2,1,0:T(8,128)(2,1)}), bf16[4,64,256]{2,1,0:T(8,128)(2,1)}) %all-reduce.2.cloned.1.call-update) | async-done | bytes 131088 | tf_op jit(solution)/shard_map/psum | solution.py:88
  279.0 4.7 %fusion = bf16[512,2048]{1,0:T(8,128)(2,1)} fusion(f32[512,2048]{1,0:T(8,128)} %fusion.24, bf16[4,128,2048]{2,1,0:T(8,128)(2,1)S(1)} %copy-done, f32[4,64]{1,0:T(4,128)S(1)} %select_reduce_fusion, f32[4,512]{1,0:T(4,128)S(1)} %get-tuple-element.9, bf16[4,64,256]{2,1,0:T(8,128)(2,1)} %all-reduce.2.cloned.1.call-done), kind=kOutput, calls=%fused_computation.4 | convolution fusion | flops 674365440 | bytes 8463360 | tf_op jit(solution)/shard_map/dot_general | solution.py:95
  283.7 0.9 copy-done.5
  284.6 2.2 convolution_convert_fusion.3
  286.8 2.1 convolution_convert_fusion.2
  288.8 63.5 %reduce-scatter.5.cloned.1.call-done = bf16[64,2048]{1,0:T(8,128)(2,1)} async-done(((bf16[512,2048]{1,0:T(8,128)(2,1)}), bf16[64,2048]{1,0:T(8,128)(2,1)}) %reduce-scatter.5.cloned.1.call-update) | async-done | bytes 262160 | tf_op jit(solution)/shard_map/reduce_scatter | solution.py:97
  (55 shorter events, 2.9 us)
Async XLA Ops:
  7.2 207.7 %copy-start = (bf16[4,128,2048]{2,1,0:T(8,128)(2,1)S(1)}, bf16[4,128,2048]{2,1,0:T(8,128)(2,1)}, u32[]{:S(2)}) copy-start(bf16[4,128,2048]{2,1,0:T(8,128)(2,1)} %param.14) | copy-start | bytes 6291460
  7.2 54.8 %all-gather.4.cloned.1.call-start = ((), (), s32[]{:S(2)}) async-start(), calls=%async_computation.2 | async-start | bytes 2359296 | tf_op jit(solution)/shard_map/all_gather | solution.py:43
  7.9 152.9 %reduce-scatter.3.cloned.1.call-start = ((), (), s32[]{:S(2)}) async-start(), calls=%async_computation.3 | async-start | bytes 9175040 | tf_op jit(solution)/shard_map/reduce_scatter | solution.py:18
  62.0 15.0 %copy-start.4 = (bf16[512,2048]{1,0:T(8,128)(2,1)S(1)}, bf16[512,2048]{1,0:T(8,128)(2,1)}, u32[]{:S(2)}) copy-start(bf16[512,2048]{1,0:T(8,128)(2,1)} %all-gather.4.cloned.1.call-done) | copy-start | bytes 6291460
  96.2 116.4 %all-gather.8.cloned.1.call-start = ((), (), s32[]{:S(2)}) async-start(), calls=%async_computation.5 | async-start | bytes 2359296 | tf_op jit(solution)/shard_map/all_gather | solution.py:56
  96.9 147.5 %all-gather.6.cloned.1.call-start = ((), (), s32[]{:S(2)}) async-start(), calls=%async_computation.4 | async-start | bytes 4587520 | tf_op jit(solution)/shard_map/all_gather | solution.py:22
  162.7 1.5 copy-start.6
  162.7 1.5 copy-start.7
  164.2 114.8 %all-reduce.2.cloned.1.call-start = ((), (), s32[]{:S(2)}) async-start(), calls=%async_computation.6 | async-start | bytes 262144 | tf_op jit(solution)/shard_map/psum | solution.py:88
  164.3 6.3 %collective-permute-start = (f32[4,64]{1,0:T(4,128)S(1)}, f32[4,64]{1,0:T(4,128)S(1)}, u32[]{:S(2)}, u32[]{:S(2)}) collective-permute-start(f32[4,64]{1,0:T(4,128)S(1)} %pad_maximum_fusion.2), channel_id=1, source_target_pairs={{0,4},{4,8},{8,12},{12,16},{16,20},{20,24},{24,28},{28,0},{1,5},{5... | collective-permute-start | bytes 3080 | tf_op jit(solution)/shard_map/ppermute | solution.py:52
  170.6 6.3 %collective-permute-start.1 = (f32[4,64]{1,0:T(4,128)S(1)}, f32[4,64]{1,0:T(4,128)S(1)}, u32[]{:S(2)}, u32[]{:S(2)}) collective-permute-start(f32[4,64]{1,0:T(4,128)S(1)} %collective-permute-done), channel_id=1, source_target_pairs={{0,4},{4,8},{8,12},{12,16},{16,20},{20,24},{24,28},{28,0},{1,5},{5... | collective-permute-start | bytes 3080 | tf_op jit(solution)/shard_map/ppermute | solution.py:52
  176.9 6.3 %collective-permute-start.2 = (f32[4,64]{1,0:T(4,128)S(1)}, f32[4,64]{1,0:T(4,128)S(1)}, u32[]{:S(2)}, u32[]{:S(2)}) collective-permute-start(f32[4,64]{1,0:T(4,128)S(1)} %collective-permute-done.1), channel_id=1, source_target_pairs={{0,4},{4,8},{8,12},{12,16},{16,20},{20,24},{24,28},{28,0},{1,5},{5... | collective-permute-start | bytes 3080 | tf_op jit(solution)/shard_map/ppermute | solution.py:52
  183.2 6.3 %collective-permute-start.3 = (f32[4,64]{1,0:T(4,128)S(1)}, f32[4,64]{1,0:T(4,128)S(1)}, u32[]{:S(2)}, u32[]{:S(2)}) collective-permute-start(f32[4,64]{1,0:T(4,128)S(1)} %collective-permute-done.2), channel_id=1, source_target_pairs={{0,4},{4,8},{8,12},{12,16},{16,20},{20,24},{24,28},{28,0},{1,5},{5... | collective-permute-start | bytes 3080 | tf_op jit(solution)/shard_map/ppermute | solution.py:52
  189.5 6.3 %collective-permute-start.4 = (f32[4,64]{1,0:T(4,128)S(1)}, f32[4,64]{1,0:T(4,128)S(1)}, u32[]{:S(2)}, u32[]{:S(2)}) collective-permute-start(f32[4,64]{1,0:T(4,128)S(1)} %collective-permute-done.3), channel_id=1, source_target_pairs={{0,4},{4,8},{8,12},{12,16},{16,20},{20,24},{24,28},{28,0},{1,5},{5... | collective-permute-start | bytes 3080 | tf_op jit(solution)/shard_map/ppermute | solution.py:52
  195.8 6.5 %collective-permute-start.5 = (f32[4,64]{1,0:T(4,128)S(1)}, f32[4,64]{1,0:T(4,128)S(1)}, u32[]{:S(2)}, u32[]{:S(2)}) collective-permute-start(f32[4,64]{1,0:T(4,128)S(1)} %collective-permute-done.4), channel_id=1, source_target_pairs={{0,4},{4,8},{8,12},{12,16},{16,20},{20,24},{24,28},{28,0},{1,5},{5... | collective-permute-start | bytes 3080 | tf_op jit(solution)/shard_map/ppermute | solution.py:52
  202.2 6.3 %collective-permute-start.6 = (f32[4,64]{1,0:T(4,128)S(1)}, f32[4,64]{1,0:T(4,128)S(1)}, u32[]{:S(2)}, u32[]{:S(2)}) collective-permute-start(f32[4,64]{1,0:T(4,128)S(1)} %collective-permute-done.5), channel_id=1, source_target_pairs={{0,4},{4,8},{8,12},{12,16},{16,20},{20,24},{24,28},{28,0},{1,5},{5... | collective-permute-start | bytes 3080 | tf_op jit(solution)/shard_map/ppermute | solution.py:52
  214.9 2.5 copy-start.1
  214.9 2.0 copy-start.3
  218.1 134.2 %reduce-scatter.5.cloned.1.call-start = ((), (), s32[]{:S(2)}) async-start(), calls=%async_computation.7 | async-start | bytes 2359296 | tf_op jit(solution)/shard_map/reduce_scatter | solution.py:97
  283.6 0.9 copy-start.5
  284.6 2.2 copy-start.2
Sparse Core Ops, SparseCore 0:
  10.1 51.7 all-gather.3
  96.3 64.4 reduce-scatter.2
  163.0 49.5 all-gather.7
  214.5 29.8 all-gather.5
  247.2 31.7 all-reduce.1
  283.8 68.4 reduce-scatter.4
